TPU v7x, 256 devices: a whole 4x4x8 slice. The times are simulated.
256 devices in a mesh: row: 32 (over x_lo, z, core), col: 8 (over y, x_hi).
Axes of the slice: x: 4 (x_hi: 2, x_lo: 2; x = x_hi * 2 + x_lo), y: 4, z: 8, core: 2. Of those that a mesh axis runs over, the one named last changes fastest.
Arguments:
- hessian: float32 [14336, 14336], P('row', 'col'), may hold values from -1 to 6, as said below
- dense_weight: float32 [14336, 1024], P('col', 'row'), may hold values from -6 to 6
- start_iterate: float32 [14336, 1024], P('col', 'row'), may hold values from -6 to 6
- start_multiplier: float32 [14336, 1024], P('col', 'row'), may hold values from -3 to 3
- keep_mask: int32 [14336, 1024], P('col', 'row'), may hold values 0 or 1
Outputs:
- iterate: float32 [14336, 1024], P('col', 'row')
- projected: float32 [14336, 1024], P('col', 'row')
- multiplier: float32 [14336, 1024], P('col', 'row')
Inputs may be any that keep to these rules, and one draw needn't show every extreme that they name: `hessian`: a calibration Hessian: symmetric up to rounding and positive definite.
All inputs are finite; a program needn't handle non-finite values. No bound on the sum of `keep_mask` on one device may be relied on, other than what follows from the above.
Results may differ from a plain program's by a relative error of at most 0.0001.
Values sent between devices are 32-bit elements; how exact they have to be, the bound alone decides.
A program may use at most 64 MiB of HBM per device.

v0:
```python
import jax
import jax.numpy as jnp
from jax import lax
from jax.sharding import PartitionSpec as P

ITERS = 2
step_size = 0.25
penalty = 1.0


def split_up(array, dim, length):
    before, after = (array.shape[:dim], array.shape[dim + 1 :])
    return jnp.moveaxis(array.reshape(*before, length, -1, *after), dim, 0)


def sum_at_owner(array, axis, dim):
    tiles = split_up(array, dim, lax.axis_size(axis))
    arrived = lax.all_to_all(tiles, axis, split_axis=0, concat_axis=0, tiled=True)
    return arrived.sum(axis=0)


def per_device(hessian, dense_weight, start_iterate, start_multiplier, keep_mask):
    keeping = keep_mask.astype(jnp.float32)
    iterate = start_iterate
    multiplier = start_multiplier
    projected = keeping * (iterate + multiplier)
    for rounds in range(ITERS):
        change = iterate - dense_weight
        gathered = lax.all_gather(change, "row", axis=1, tiled=True)
        partial_value = jnp.dot(
            hessian, gathered, precision=lax.Precision.HIGHEST, preferred_element_type=jnp.float32
        )
        summed = sum_at_owner(partial_value, "col", 0)
        shaped = summed.reshape(1, 1, summed.shape[0], summed.shape[1])
        relaid = lax.all_to_all(
            lax.all_to_all(shaped, "row", split_axis=3, concat_axis=0, tiled=True),
            "col",
            split_axis=0,
            concat_axis=1,
            tiled=True,
        )
        gradient = relaid.reshape(iterate.shape)
        iterate = iterate - step_size * (gradient + penalty * (iterate - projected + multiplier))
        projected = keeping * (iterate + multiplier)
        multiplier = multiplier + iterate - projected
    return (iterate, projected, multiplier)


def solution(mesh):
    return jax.shard_map(
        per_device,
        mesh=mesh,
        in_specs=(
            P("row", "col"),
            P("col", "row"),
            P("col", "row"),
            P("col", "row"),
            P("col", "row"),
        ),
        out_specs=(P("col", "row"), P("col", "row"), P("col", "row")),
        check_vma=False,
    )
```

profile of v0, /device:TPU:2, one launch (start us, length us, event | category | flops | bytes accessed | tf_op | source)
XLA Modules:
  0.0 363.2 jit_solution(16763132833857299460)
XLA Ops:
  9.2 75.1 %all-gather.3.cloned.1.call-done = f32[1792,1024]{0,1:T(8,128)} async-done(((f32[1792,32]{0,1:T(8,128)}), f32[1792,1024]{0,1:T(8,128)}) %all-gather.3.cloned.1.call-update) | async-done | bytes 7340048 | tf_op jit(solution)/shard_map/all_gather | solution.py:29
  84.3 12.9 %fusion.4 = f32[1024,448]{0,1:T(8,128)S(1)} fusion(f32[1792,1024]{0,1:T(8,128)} %all-gather.3.cloned.1.call-done, f32[448,1792]{1,0:T(8,128)S(1)} %copy-done), kind=kOutput, calls=%fused_computation.8 | convolution fusion | flops 9865003008 | bytes 12386304 | tf_op jit(solution)/shard_map/dot_general | solution.py:30
  97.2 31.7 %all_to_all.76 = f32[8,56,1024]{2,1,0:T(8,128)} all-to-all(f32[8,56,1024]{2,1,0:T(8,128)S(1)} %bitcast.54), channel_id=1, replica_groups=mesh['row'=32,'col'=8] {'col'}, dimensions={0} | all-to-all | bytes 3670016 | tf_op jit(solution)/shard_map/all_to_all | solution.py:18
  132.1 3.8 %reduce = f32[1024,56]{1,0:T(8,128)} reduce(f32[1024,1,1,56]{3,2,1,0:T(1,128)} %bitcast.48, f32[]{:T(128)} %broadcast.8), dimensions={1,2}, to_apply=%bitcast.36.reduce_sub_computation | reduce | bytes 458756
  135.9 2.3 reshape.32
  138.2 18.4 %all_to_all.77 = f32[32,1,1792]{2,1,0:T(1,128)} all-to-all(f32[32,1,1792]{2,1,0:T(1,128)} %reshape.32), channel_id=1, replica_groups=mesh['row'=32,'col'=8] {'row'}, dimensions={0} | all-to-all | bytes 458752 | tf_op jit(solution)/shard_map/all_to_all | solution.py:36
  156.6 2.8 reduce.1
  159.4 2.8 reshape.33
  162.2 2.3 reshape.34
  164.4 12.6 %all_to_all.78 = f32[8,1,7168]{2,1,0:T(1,128)} all-to-all(f32[8,1,7168]{2,1,0:T(1,128)} %reshape.34), channel_id=1, replica_groups=mesh['row'=32,'col'=8] {'col'}, dimensions={0} | all-to-all | bytes 458752 | tf_op jit(solution)/shard_map/all_to_all | solution.py:35
  177.1 2.8 reduce.2
  179.9 2.2 reshape.35
  188.4 64.4 %all-gather.5.cloned.1.call-done = f32[1792,1024]{0,1:T(8,128)} async-done(((f32[1792,32]{0,1:T(8,128)}), f32[1792,1024]{0,1:T(8,128)}) %all-gather.5.cloned.1.call-update) | async-done | bytes 7340048 | tf_op jit(solution)/shard_map/all_gather | solution.py:29
  252.8 12.9 %fusion.5 = f32[1024,448]{0,1:T(8,128)S(1)} fusion(f32[1792,1024]{0,1:T(8,128)} %all-gather.5.cloned.1.call-done, f32[448,1792]{1,0:T(8,128)S(1)} %copy-done), kind=kOutput, calls=%fused_computation.9 | convolution fusion | flops 9865003008 | bytes 12386304 | tf_op jit(solution)/shard_map/dot_general | solution.py:30
  265.7 31.7 %all_to_all.79 = f32[8,56,1024]{2,1,0:T(8,128)} all-to-all(f32[8,56,1024]{2,1,0:T(8,128)S(1)} %bitcast.55), channel_id=1, replica_groups=mesh['row'=32,'col'=8] {'col'}, dimensions={0} | all-to-all | bytes 3670016 | tf_op jit(solution)/shard_map/all_to_all | solution.py:18
  300.1 3.8 %reduce.3 = f32[1024,56]{1,0:T(8,128)} reduce(f32[1024,1,1,56]{3,2,1,0:T(1,128)} %bitcast.51, f32[]{:T(128)} %broadcast.8), dimensions={1,2}, to_apply=%bitcast.40.reduce_sub_computation | reduce | bytes 458756
  303.9 2.3 reshape.36
  306.2 18.4 %all_to_all.80 = f32[32,1,1792]{2,1,0:T(1,128)} all-to-all(f32[32,1,1792]{2,1,0:T(1,128)} %reshape.36), channel_id=1, replica_groups=mesh['row'=32,'col'=8] {'row'}, dimensions={0} | all-to-all | bytes 458752 | tf_op jit(solution)/shard_map/all_to_all | solution.py:36
  324.6 2.8 reduce.4
  327.4 2.8 reshape.37
  330.2 2.3 reshape.38
  332.4 12.6 %all_to_all.81 = f32[8,1,7168]{2,1,0:T(1,128)} all-to-all(f32[8,1,7168]{2,1,0:T(1,128)} %reshape.38), channel_id=1, replica_groups=mesh['row'=32,'col'=8] {'col'}, dimensions={0} | all-to-all | bytes 458752 | tf_op jit(solution)/shard_map/all_to_all | solution.py:35
  345.1 2.8 reduce.5
  347.9 2.2 reshape.39
  (22 shorter events, 20.4 us)
Async XLA Ops:
  7.2 77.1 %copy-start = (f32[448,1792]{1,0:T(8,128)S(1)}, f32[448,1792]{1,0:T(8,128)}, u32[]{:S(2)}) copy-start(f32[448,1792]{1,0:T(8,128)} %param.5) | copy-start | bytes 9633796
  7.2 77.1 %all-gather.3.cloned.1.call-start = ((), (), s32[]{:S(2)}) async-start(), calls=%async_computation.6 | async-start | bytes 7569408 | tf_op jit(solution)/shard_map/all_gather | solution.py:29
  9.2 243.6 %all-gather.5.cloned.1.call-start = ((), (), s32[]{:S(2)}) async-start(), calls=%async_computation.7 | async-start | bytes 7569408 | tf_op jit(solution)/shard_map/all_gather | solution.py:29
  135.9 50.3 %copy-start.1 = (s32[1792,32]{0,1:T(8,128)S(1)}, s32[1792,32]{0,1:T(8,128)}, u32[]{:S(2)}) copy-start(s32[1792,32]{0,1:T(8,128)} %param.9) | copy-start | bytes 688132
  303.9 50.3 %copy-start.2 = (s32[1792,32]{0,1:T(8,128)S(1)}, s32[1792,32]{0,1:T(8,128)}, u32[]{:S(2)}) copy-start(s32[1792,32]{0,1:T(8,128)} %param.9) | copy-start | bytes 688132
Sparse Core Ops, SparseCore 0:
  10.4 73.8 all-gather.2
  188.5 64.2 all-gather.4
where the time goes:
time: 364 us; the launch traced here: 363 us
  waiting for transfers between devices  140 us (38%)
  blocking collectives  125 us (34%)
  local copies, waits for them, and re-layouts  29.9 us (8%)
  other arithmetic  28.2 us (8%)
  matrix products  25.8 us (7%)
  between operations  14.1 us (4%)
    all_gather x2, waiting for transfers between devices, per_device(): gathered = lax.all_gather(change, 'row', axis=1, tiled=True)  139 us
    all_to_all x2, blocking collectives, sum_at_owner(): lax.all_to_all(tiles, axis, split_axis=0, concat_axis=0, tiled=True)  63.5 us
    all_to_all x2, blocking collectives, per_device(): lax.all_to_all(shaped, 'row', split_axis=3, concat_axis=0, tiled=True)  36.8 us
    dot_general x2, matrix products, per_device(): jnp.dot(hessian, gathered, precision=lax.Precision.HIGHEST, preferred_ele...  25.8 us
    all_to_all x2, blocking collectives, per_device(): lax.all_to_all(lax.all_to_all(shaped, 'row', split_axis=3, concat_axis=0,...  25.3 us
    unnamed x15, local copies, waits for them, and re-layouts  19.6 us
    unnamed x2, other arithmetic  7.59 us
  transfers between devices with their start and end apart: 2, of which 2 were waited for; matrix products, arithmetic and copies ran while one was open for 0% of the time, Pallas kernels for 0%

commit v1 on v0

--- a/solution.py
+++ b/solution.py
@@ -26,7 +26,10 @@
     projected = keeping * (iterate + multiplier)
     for rounds in range(ITERS):
         change = iterate - dense_weight
-        gathered = lax.all_gather(change, "row", axis=1, tiled=True)
+        n_dev = lax.axis_size("row")
+        shards = jnp.stack([change for _ in range(n_dev)])
+        shards = lax.all_to_all(shards, "row", split_axis=0, concat_axis=0)
+        gathered = jnp.concatenate(shards, axis=1)
         partial_value = jnp.dot(
             hessian, gathered, precision=lax.Precision.HIGHEST, preferred_element_type=jnp.float32
         )

time: 364 us -> 548 us (1.51); the launches traced: 363 us -> 539 us
  blocking collectives: 125 us -> 458 us
  waiting for transfers between devices: 140 us -> 0 us
  between operations: 14.1 us -> 0.92 us
    all_to_all x0 -> x2, blocking collectives: none -> 339 us  [per_device(): shards = lax.all_to_all(shards, 'row', split_axis=0, concat_axis=0)]
    all_gather x2 -> x0, waiting for transfers between devices: 139 us -> none  [per_device(): gathered = lax.all_gather(change, 'row', axis=1, tiled=True)]
  transfers between devices with their start and end apart: 2 -> 0, of which waited for: 2 -> 0; matrix products, arithmetic and copies ran while one was open for 0% -> 0% of each run, Pallas kernels for 0% -> 0%
where the time goes in v1:
time: 548 us; the launch traced here: 539 us
  blocking collectives  458 us (84%)
  local copies, waits for them, and re-layouts  31.6 us (6%)
  other arithmetic  27.5 us (5%)
  matrix products  20.7 us (4%)
    all_to_all x2, blocking collectives, per_device(): shards = lax.all_to_all(shards, 'row', split_axis=0, concat_axis=0)  339 us
    all_to_all x2, blocking collectives, sum_at_owner(): lax.all_to_all(tiles, axis, split_axis=0, concat_axis=0, tiled=True)  60 us
    all_to_all x2, blocking collectives, per_device(): lax.all_to_all(shaped, 'row', split_axis=3, concat_axis=0, tiled=True)  33.9 us
    all_to_all x2, blocking collectives, per_device(): lax.all_to_all(lax.all_to_all(shaped, 'row', split_axis=3, concat_axis=0,...  25.3 us
    dot_general x2, matrix products, per_device(): jnp.dot(hessian, gathered, precision=lax.Precision.HIGHEST, preferred_ele...  20.7 us
    unnamed x15, local copies, waits for them, and re-layouts  19.6 us

profile of v1, /device:TPU:2, one launch (start us, length us, event | category | flops | bytes accessed | tf_op | source)
XLA Modules:
  0.0 538.5 jit_solution(16623669731851044670)
XLA Ops:
  2.7 172.1 %all_to_all.86 = f32[32,1792,32]{1,2,0:T(8,128)S(1)} all-to-all(f32[32,1792,32]{1,2,0:T(8,128)S(1)} %stack.4), channel_id=1, replica_groups=mesh['row'=32,'col'=8] {'row'}, dimensions={0} | all-to-all | bytes 14680064 | tf_op jit(solution)/shard_map/all_to_all | solution.py:31
  174.8 10.3 %fusion.4 = f32[1024,448]{0,1:T(8,128)S(1)} fusion(f32[1792,1024]{0,1:T(8,128)S(1)} %bitcast.54, f32[448,1792]{1,0:T(8,128)S(1)} %copy-done), kind=kOutput, calls=%fused_computation.8 | convolution fusion | flops 9865003008 | bytes 12386304 | tf_op jit(solution)/shard_map/dot_general | solution.py:33
  185.1 31.0 %all_to_all.87 = f32[8,56,1024]{2,1,0:T(8,128)} all-to-all(f32[8,56,1024]{2,1,0:T(8,128)S(1)} %bitcast.62), channel_id=1, replica_groups=mesh['row'=32,'col'=8] {'col'}, dimensions={0} | all-to-all | bytes 3670016 | tf_op jit(solution)/shard_map/all_to_all | solution.py:18
  219.3 3.8 reduce
  223.1 2.3 reshape.52
  225.4 17.1 %all_to_all.88 = f32[32,1,1792]{2,1,0:T(1,128)} all-to-all(f32[32,1,1792]{2,1,0:T(1,128)} %reshape.52), channel_id=1, replica_groups=mesh['row'=32,'col'=8] {'row'}, dimensions={0} | all-to-all | bytes 458752 | tf_op jit(solution)/shard_map/all_to_all | solution.py:39
  242.4 2.8 reduce.1
  245.3 2.8 reshape.53
  248.0 2.3 reshape.54
  250.3 12.6 %all_to_all.89 = f32[8,1,7168]{2,1,0:T(1,128)} all-to-all(f32[8,1,7168]{2,1,0:T(1,128)} %reshape.54), channel_id=1, replica_groups=mesh['row'=32,'col'=8] {'col'}, dimensions={0} | all-to-all | bytes 458752 | tf_op jit(solution)/shard_map/all_to_all | solution.py:38
  262.9 2.8 reduce.2
  265.7 2.2 reshape.55
  275.0 166.6 %all_to_all.90 = f32[32,1792,32]{1,2,0:T(8,128)S(1)} all-to-all(f32[32,1792,32]{1,2,0:T(8,128)S(1)} %stack.5), channel_id=1, replica_groups=mesh['row'=32,'col'=8] {'row'}, dimensions={0} | all-to-all | bytes 14680064 | tf_op jit(solution)/shard_map/all_to_all | solution.py:31
  441.6 10.3 %fusion.5 = f32[1024,448]{0,1:T(8,128)S(1)} fusion(f32[1792,1024]{0,1:T(8,128)S(1)} %bitcast.55, f32[448,1792]{1,0:T(8,128)S(1)} %copy-done), kind=kOutput, calls=%fused_computation.9 | convolution fusion | flops 9865003008 | bytes 12386304 | tf_op jit(solution)/shard_map/dot_general | solution.py:33
  452.0 29.0 %all_to_all.91 = f32[8,56,1024]{2,1,0:T(8,128)} all-to-all(f32[8,56,1024]{2,1,0:T(8,128)S(1)} %bitcast.63), channel_id=1, replica_groups=mesh['row'=32,'col'=8] {'col'}, dimensions={0} | all-to-all | bytes 3670016 | tf_op jit(solution)/shard_map/all_to_all | solution.py:18
  483.6 3.8 reduce.3
  487.4 2.3 reshape.56
  489.7 16.8 %all_to_all.92 = f32[32,1,1792]{2,1,0:T(1,128)} all-to-all(f32[32,1,1792]{2,1,0:T(1,128)} %reshape.56), channel_id=1, replica_groups=mesh['row'=32,'col'=8] {'row'}, dimensions={0} | all-to-all | bytes 458752 | tf_op jit(solution)/shard_map/all_to_all | solution.py:39
  506.6 2.8 reduce.4
  509.4 2.8 reshape.57
  512.2 2.3 reshape.58
  514.4 12.6 %all_to_all.93 = f32[8,1,7168]{2,1,0:T(1,128)} all-to-all(f32[8,1,7168]{2,1,0:T(1,128)} %reshape.58), channel_id=1, replica_groups=mesh['row'=32,'col'=8] {'col'}, dimensions={0} | all-to-all | bytes 458752 | tf_op jit(solution)/shard_map/all_to_all | solution.py:38
  527.0 2.8 reduce.5
  529.9 2.2 reshape.59
  (20 shorter events, 21.2 us)
Async XLA Ops:
  0.6 174.2 %copy-start = (f32[448,1792]{1,0:T(8,128)S(1)}, f32[448,1792]{1,0:T(8,128)}, u32[]{:S(2)}) copy-start(f32[448,1792]{1,0:T(8,128)} %param.5) | copy-start | bytes 9633796
  223.1 49.0 %copy-start.1 = (s32[1792,32]{0,1:T(8,128)S(1)}, s32[1792,32]{0,1:T(8,128)}, u32[]{:S(2)}) copy-start(s32[1792,32]{0,1:T(8,128)} %param.9) | copy-start | bytes 688132
  487.4 48.8 %copy-start.2 = (s32[1792,32]{0,1:T(8,128)S(1)}, s32[1792,32]{0,1:T(8,128)}, u32[]{:S(2)}) copy-start(s32[1792,32]{0,1:T(8,128)} %param.9) | copy-start | bytes 688132
